TPU v7x, 32 devices: a whole 2x2x4 slice. The times are simulated.
32 devices in a mesh: rep: 4 (over y, x), shard: 8 (over z, core).
Axes of the slice: x: 2, y: 2, z: 4, core: 2. Of those that a mesh axis runs over, the one named last changes fastest.
Arguments:
- inputs: bfloat16 [32768, 1024], P(('rep', 'shard')), may hold values from -6 to 6
- query_weight: bfloat16 [1024, 256], P('shard'), may hold values from -0.1875 to 0.1875
- key_weight: bfloat16 [1024, 256], P('shard'), may hold values from -0.1875 to 0.1875
- value_weight: bfloat16 [1024, 1024], P('shard'), may hold values from -0.1875 to 0.1875
- out_weight: bfloat16 [1024, 1024], P('shard'), may hold values from -6 to 6
- gate_weight: bfloat16 [1024, 2752], P('shard'), may hold values from -0.1875 to 0.1875
- up_weight: bfloat16 [1024, 2752], P('shard'), may hold values from -0.1875 to 0.1875
- down_weight: bfloat16 [1024, 2752], P('shard'), may hold values from -0.109375 to 0.109375
- attn_gain: bfloat16 [1024], P('shard'), may hold values from 0.25 to 1.75
- mlp_gain: bfloat16 [1024], P('shard'), may hold values from 0.25 to 1.75
- slot_of: int32 [4, 8], P('rep'), may hold values from 0 to 7, each once within a row
- parent_of: int32 [4, 8], P('rep'), may hold values from 0 to 1, as said below
- cotangent: bfloat16 [32768, 1024], P(('rep', 'shard')), may hold values from -6 to 6
Outputs:
- block_out: bfloat16 [32768, 1024], P(('rep', 'shard'))
- input_grad: float32 [32768, 1024], P(('rep', 'shard'))
- query_grad: float32 [1024, 256], P('shard')
- key_grad: float32 [1024, 256], P('shard')
- value_grad: float32 [1024, 1024], P('shard')
- out_grad: float32 [1024, 1024], P('shard')
- gate_grad: float32 [1024, 2752], P('shard')
- up_grad: float32 [1024, 2752], P('shard')
- down_grad: float32 [1024, 2752], P('shard')
- attn_gain_grad: float32 [1024], P('shard')
- mlp_gain_grad: float32 [1024], P('shard')
Inputs may be any that keep to these rules, and one draw needn't show every extreme that they name: `slot_of`: each row is a permutation of the slots of its group. `parent_of`: each row names each of the 2 families for exactly 4 continuations.
All inputs are finite; a program needn't handle non-finite values.
Results may differ from a plain program's by a relative error of at most 0.02.
Values may be sent and summed in bfloat16 or wider, within the bound.
No kernel may reach another device: no remote copies, remote signals or barrier semaphores. Data moves between devices by JAX's collectives and lax.ppermute only.
A program may use at most 320 MiB of HBM per device.

v0:
```python
from functools import partial
import math
import jax
import jax.numpy as jnp
from jax import lax
from jax.sharding import PartitionSpec as P

HEADS = 16
CONT_PER = 4
norm_eps = 1e-05


def on_whole(value, axis, dim, block):
    whole = lax.all_gather(value, axis, axis=dim, tiled=True)
    return block(whole, jnp.int32(0))


def features(vectors):
    width = vectors.shape[-1]
    square = vectors[..., :, None] * vectors[..., None, :]
    square = square.reshape(vectors.shape[:-1] + (width * width,))
    return jnp.concatenate(
        [
            jnp.ones_like(vectors[..., :1]),
            vectors / width**0.25,
            square / (math.sqrt(2.0) * math.sqrt(width)),
        ],
        axis=-1,
    )


def contract_last(left, right):
    return lax.dot_general(
        left, right, (((1,), (1,)), ((), ())), preferred_element_type=jnp.float32
    )


def contract_first(left, right):
    return lax.dot_general(
        left, right, (((0,), (0,)), ((), ())), preferred_element_type=jnp.float32
    )


def group_heads(values):
    rows_count, heads_count, inner_dim = values.shape
    return values.reshape(rows_count, heads_count // 4, 4, inner_dim).transpose(1, 0, 2, 3)


def group_plain(values):
    rows_count, heads_count = values.shape
    return values.reshape(rows_count, heads_count // 4, 4).transpose(1, 0, 2)


def ungroup_heads(values):
    block_count, rows_count, block_heads, inner_dim = values.shape
    return values.transpose(1, 0, 2, 3).reshape(rows_count, block_count * block_heads, inner_dim)


def ungroup_plain(values):
    block_count, rows_count, block_heads = values.shape
    return values.transpose(1, 0, 2).reshape(rows_count, block_count * block_heads)


def kernel_of(queries, key_heads, allowed):
    scores = jnp.einsum(
        "thf,uhf->htu", queries, key_heads, preferred_element_type=jnp.float32
    ) / math.sqrt(queries.shape[-1])
    kernel = jnp.where(allowed[None], 1.0 + scores + 0.5 * scores * scores, 0.0)
    return (scores, kernel)


def local_forward(allowed, blocks):
    queries, key_heads, value_heads = blocks
    scores, kernel = kernel_of(queries, key_heads, allowed)
    numerator = jnp.einsum(
        "htu,uhe->the", kernel.astype(jnp.bfloat16), value_heads, preferred_element_type=jnp.float32
    )
    denominator = jnp.sum(kernel, axis=2).T
    return (numerator, denominator)


def local_backward(allowed, blocks):
    queries, key_heads, value_heads, grad_num, grad_den = blocks
    scores, kernel = kernel_of(queries, key_heads, allowed)
    grad_kernel = (
        jnp.einsum("the,uhe->htu", grad_num, value_heads, preferred_element_type=jnp.float32)
        + grad_den.T.astype(jnp.float32)[:, :, None]
    )
    grad_scores = (jnp.where(allowed[None], grad_kernel, 0.0) * (1.0 + scores)).astype(jnp.bfloat16)
    root = math.sqrt(queries.shape[-1])
    grad_query = (
        jnp.einsum("htu,uhf->thf", grad_scores, key_heads, preferred_element_type=jnp.float32)
        / root
    )
    grad_key = (
        jnp.einsum("htu,thf->uhf", grad_scores, queries, preferred_element_type=jnp.float32) / root
    )
    grad_value = jnp.einsum(
        "htu,the->uhe", kernel.astype(jnp.bfloat16), grad_num, preferred_element_type=jnp.float32
    )
    return (grad_query, grad_key, grad_value)


def local(
    inputs,
    query_weight,
    key_weight,
    value_weight,
    out_weight,
    gate_weight,
    up_weight,
    down_weight,
    attn_gain,
    mlp_gain,
    slot_of,
    parent_of,
    cotangent,
):
    tok_rows, width = inputs.shape
    half_rows = tok_rows // 2
    qk_width = query_weight.shape[1]
    value_width = value_weight.shape[1]
    hidden_width = gate_weight.shape[1]
    state_rows = value_width + HEADS
    shards = lax.axis_size("shard")
    own_index = lax.axis_index("shard")
    slot_ids = slot_of[0]
    parent_ids = parent_of[0]
    prompt_slots = shards // 2
    pieces_per = CONT_PER // 2
    own_slot = lax.dynamic_index_in_dim(slot_ids, own_index, keepdims=False)
    own_prompt = own_slot < prompt_slots
    source_prompt = slot_ids < prompt_slots
    source_family = slot_ids // pieces_per
    earlier = (
        source_prompt
        & (source_family == own_slot // pieces_per)
        & (slot_ids % pieces_per < own_slot % pieces_per)
    )
    pair_index = jnp.clip(own_slot - prompt_slots, 0, shards // 2 - 1)
    first_parent = lax.dynamic_index_in_dim(parent_ids, 2 * pair_index, keepdims=False)
    second_parent = lax.dynamic_index_in_dim(parent_ids, 2 * pair_index + 1, keepdims=False)
    from_first = source_prompt & (source_family == first_parent)
    from_second = source_prompt & (source_family == second_parent)
    source_mix = jnp.where(
        own_prompt, jnp.stack([earlier, earlier]), jnp.stack([from_first, from_second])
    ).astype(jnp.float32)
    positions = lax.broadcasted_iota(jnp.int32, (tok_rows,), 0)
    segment_ids = jnp.where(own_prompt, 0, positions // half_rows)
    allowed = (positions[None, :] <= positions[:, None]) & (
        segment_ids[None, :] == segment_ids[:, None]
    )
    x_float = inputs.astype(jnp.float32)
    inv_one = lax.rsqrt(jnp.mean(x_float * x_float, axis=1, keepdims=True) + norm_eps)
    norm_one = x_float * inv_one
    part_query = lax.all_gather(query_weight, "shard", axis=0, tiled=True)
    part_key = lax.all_gather(key_weight, "shard", axis=0, tiled=True)
    part_value = lax.all_gather(value_weight, "shard", axis=0, tiled=True)
    part_gain = lax.all_gather(attn_gain, "shard", axis=0, tiled=True)
    scaled = (norm_one * part_gain.astype(jnp.float32)).astype(jnp.bfloat16)
    acc_query = jnp.dot(scaled, part_query, preferred_element_type=jnp.float32)
    acc_key = jnp.dot(scaled, part_key, preferred_element_type=jnp.float32)
    acc_value = jnp.dot(scaled, part_value, preferred_element_type=jnp.float32)
    hidden_one = scaled
    gain_one = part_gain
    queries = acc_query.astype(jnp.bfloat16).reshape(tok_rows, HEADS, -1)
    key_heads = acc_key.astype(jnp.bfloat16).reshape(tok_rows, HEADS, -1)
    value_heads = acc_value.astype(jnp.bfloat16).reshape(tok_rows, HEADS, -1)
    query_float = queries.astype(jnp.float32)
    key_float = key_heads.astype(jnp.float32)
    query_feat = features(query_float).astype(jnp.bfloat16)
    key_feat = features(key_float).astype(jnp.bfloat16)
    taylor = query_feat.shape[2]
    ones_col = jnp.ones((tok_rows,), jnp.bfloat16)
    value_state = jnp.einsum(
        "the,thf->hef", value_heads, key_feat, preferred_element_type=jnp.float32
    ).reshape(value_width, taylor)
    norm_state = jnp.einsum("t,thf->hf", ones_col, key_feat, preferred_element_type=jnp.float32)
    own_state = jnp.concatenate([value_state, norm_state], axis=0).astype(jnp.bfloat16)
    add_portion = lax.all_gather(own_state, "shard", axis=0, tiled=True)
    sources = add_portion.shape[0] // state_rows
    mix = source_mix.astype(jnp.bfloat16)
    slot_states = jnp.einsum(
        "sn,nrf->srf",
        mix,
        add_portion.reshape(sources, state_rows, taylor),
        preferred_element_type=jnp.float32,
    )
    used_states = slot_states.astype(jnp.bfloat16)
    used_values = used_states[:, :value_width].reshape(2, HEADS, -1, taylor)
    used_norms = used_states[:, value_width:]
    halves_query = query_feat.reshape(2, half_rows, HEADS, taylor)
    state_num = jnp.einsum(
        "nthf,nhef->nthe", halves_query, used_values, preferred_element_type=jnp.float32
    ).reshape(tok_rows, HEADS, -1)
    state_den = jnp.einsum(
        "nthf,nhf->nth", halves_query, used_norms, preferred_element_type=jnp.float32
    ).reshape(tok_rows, HEADS)
    local_num, local_den = lax.map(
        partial(local_forward, allowed),
        (group_heads(queries), group_heads(key_heads), group_heads(value_heads)),
    )
    numerator = ungroup_heads(local_num) + state_num
    denominator = ungroup_plain(local_den) + state_den
    ratio = numerator / denominator[:, :, None]
    mixed = ratio.reshape(tok_rows, value_width).astype(jnp.bfloat16)
    attn_out = on_whole(
        out_weight, "shard", 0, lambda portion, offset: contract_last(mixed, portion)
    )
    after_attn = x_float + attn_out
    inv_two = lax.rsqrt(jnp.mean(after_attn * after_attn, axis=1, keepdims=True) + norm_eps)
    norm_two = after_attn * inv_two
    part_gate = lax.all_gather(gate_weight, "shard", axis=0, tiled=True)
    part_up = lax.all_gather(up_weight, "shard", axis=0, tiled=True)
    part_gain = lax.all_gather(mlp_gain, "shard", axis=0, tiled=True)
    scaled = (norm_two * part_gain.astype(jnp.float32)).astype(jnp.bfloat16)
    gate_pre = jnp.dot(scaled, part_gate, preferred_element_type=jnp.float32)
    up_pre = jnp.dot(scaled, part_up, preferred_element_type=jnp.float32)
    sigma = jax.nn.sigmoid(gate_pre)
    activated = (gate_pre * sigma * up_pre).astype(jnp.bfloat16)
    mlp_out = on_whole(
        down_weight, "shard", 0, lambda portion, offset: contract_last(activated, portion)
    )
    block_out = (after_attn + mlp_out).astype(jnp.bfloat16)
    cot_float = cotangent.astype(jnp.float32)
    grad_act = jnp.dot(
        cotangent,
        lax.all_gather(down_weight, "shard", axis=0, tiled=True),
        preferred_element_type=jnp.float32,
    )
    grad_up = (grad_act * gate_pre * sigma).astype(jnp.bfloat16)
    grad_gate = (grad_act * up_pre * sigma * (1.0 + gate_pre * (1.0 - sigma))).astype(jnp.bfloat16)
    grad_hidden_two = on_whole(
        (gate_weight, up_weight),
        "shard",
        0,
        lambda portion, offset: contract_last(grad_gate, portion[0])
        + contract_last(grad_up, portion[1]),
    )
    grad_norm_two = grad_hidden_two * part_gain.astype(jnp.float32)
    grad_after = cot_float + inv_two * (
        grad_norm_two - norm_two * jnp.mean(grad_norm_two * norm_two, axis=1, keepdims=True)
    )
    grad_attn = grad_after.astype(jnp.bfloat16)
    grad_mixed = jnp.dot(
        grad_attn,
        lax.all_gather(out_weight, "shard", axis=0, tiled=True),
        preferred_element_type=jnp.float32,
    ).reshape(tok_rows, HEADS, -1)
    grad_num = (grad_mixed / denominator[:, :, None]).astype(jnp.bfloat16)
    grad_den = (-jnp.sum(grad_mixed * ratio, axis=2) / denominator).astype(jnp.bfloat16)
    local_dq, local_dk, local_dv = lax.map(
        partial(local_backward, allowed),
        (
            group_heads(queries),
            group_heads(key_heads),
            group_heads(value_heads),
            group_heads(grad_num),
            group_plain(grad_den),
        ),
    )
    halves_num = grad_num.reshape(2, half_rows, HEADS, -1)
    halves_den = grad_den.reshape(2, half_rows, HEADS)
    grad_query_feat = (
        jnp.einsum("nthe,nhef->nthf", halves_num, used_values, preferred_element_type=jnp.float32)
        + jnp.einsum("nth,nhf->nthf", halves_den, used_norms, preferred_element_type=jnp.float32)
    ).reshape(tok_rows, HEADS, taylor)
    grad_slot_values = jnp.einsum(
        "nthf,nthe->nhef", halves_query, halves_num, preferred_element_type=jnp.float32
    ).reshape(2, value_width, taylor)
    grad_slot_norms = jnp.einsum(
        "nthf,nth->nhf", halves_query, halves_den, preferred_element_type=jnp.float32
    )
    grad_slots = jnp.concatenate([grad_slot_values, grad_slot_norms], axis=1)
    mix = source_mix
    grad_state = lax.psum_scatter(
        jnp.einsum("sn,srf->nrf", mix, grad_slots, precision=lax.Precision.HIGHEST)
        .reshape(state_rows * lax.axis_size("shard"), taylor)
        .astype(jnp.bfloat16),
        "shard",
        scatter_dimension=0,
        tiled=True,
    )
    grad_value_state = grad_state[:value_width].reshape(HEADS, -1, taylor)
    grad_norm_state = grad_state[value_width:]
    grad_key_feat = (
        jnp.einsum(
            "hef,the->thf", grad_value_state, value_heads, preferred_element_type=jnp.float32
        )
        + grad_norm_state.astype(jnp.float32)[None]
    )
    value_from_state = jnp.einsum(
        "thf,hef->the", key_feat, grad_value_state, preferred_element_type=jnp.float32
    )
    query_from_feat = jax.vjp(features, query_float)[1](grad_query_feat)[0]
    key_from_feat = jax.vjp(features, key_float)[1](grad_key_feat)[0]
    grad_queries = (
        (ungroup_heads(local_dq) + query_from_feat).reshape(tok_rows, qk_width).astype(jnp.bfloat16)
    )
    grad_keys = (
        (ungroup_heads(local_dk) + key_from_feat).reshape(tok_rows, qk_width).astype(jnp.bfloat16)
    )
    grad_values = (
        (ungroup_heads(local_dv) + value_from_state)
        .reshape(tok_rows, value_width)
        .astype(jnp.bfloat16)
    )
    grad_hidden_one = on_whole(
        (query_weight, key_weight, value_weight),
        "shard",
        0,
        lambda portion, offset: contract_last(grad_queries, portion[0])
        + contract_last(grad_keys, portion[1])
        + contract_last(grad_values, portion[2]),
    )
    grad_norm_one = grad_hidden_one * gain_one.astype(jnp.float32)
    input_grad = grad_after + inv_one * (
        grad_norm_one - norm_one * jnp.mean(grad_norm_one * norm_one, axis=1, keepdims=True)
    )
    gain_term_one = grad_hidden_one * norm_one
    gain_term_two = grad_hidden_two * norm_two
    grad_qkv = jnp.concatenate([grad_queries, grad_keys, grad_values], axis=1)
    grad_gate_up = jnp.concatenate([grad_gate, grad_up], axis=1)
    pick = lambda source_array: source_array
    group_share = lax.psum_scatter(
        jnp.concatenate(
            [
                contract_first(pick(hidden_one), grad_qkv),
                contract_first(pick(grad_attn), mixed),
                contract_first(pick(scaled), grad_gate_up),
                contract_first(pick(cotangent), activated),
                jnp.sum(pick(gain_term_one), axis=0)[:, None],
                jnp.sum(pick(gain_term_two), axis=0)[:, None],
            ],
            axis=1,
        ).astype(jnp.bfloat16),
        "shard",
        scatter_dimension=0,
        tiled=True,
    )
    own_grads = lax.psum(group_share, "rep").astype(jnp.float32)
    edge_two = qk_width + qk_width
    edge_three = edge_two + value_width
    edge_four = edge_three + value_width
    edge_five = edge_four + hidden_width
    edge_six = edge_five + hidden_width
    edge_seven = edge_six + hidden_width
    return (
        block_out,
        input_grad,
        own_grads[:, :qk_width],
        own_grads[:, qk_width:edge_two],
        own_grads[:, edge_two:edge_three],
        own_grads[:, edge_three:edge_four],
        own_grads[:, edge_four:edge_five],
        own_grads[:, edge_five:edge_six],
        own_grads[:, edge_six:edge_seven],
        own_grads[:, edge_seven],
        own_grads[:, edge_seven + 1],
    )


def solution(mesh):
    placed = (
        P(("rep", "shard"), None),
        P("shard", None),
        P("shard", None),
        P("shard", None),
        P("shard", None),
        P("shard", None),
        P("shard", None),
        P("shard", None),
        P("shard"),
        P("shard"),
        P("rep", None),
        P("rep", None),
        P(("rep", "shard"), None),
    )
    return jax.shard_map(
        local,
        mesh=mesh,
        in_specs=placed,
        out_specs=(
            P(("rep", "shard"), None),
            P(("rep", "shard"), None),
            P("shard", None),
            P("shard", None),
            P("shard", None),
            P("shard", None),
            P("shard", None),
            P("shard", None),
            P("shard", None),
            P("shard"),
            P("shard"),
        ),
        check_vma=False,
    )
```

profile of v0, /device:TPU:0, one launch (start us, length us, event | category | flops | bytes accessed | tf_op | source)
XLA Modules:
  0.0 1114.8 jit_solution(6212220869168196635)
XLA Ops:
  10.9 13.5 %all-gather = bf16[8,1,128]{2,1,0:T(2,128)(2,1)S(1)} all-gather(bf16[1,1,128]{2,1,0:T(2,128)(2,1)S(1)} %bitcast.339), channel_id=1, replica_groups=mesh['rep'=4,'shard'=8] {'shard'}, dimensions={0}, use_global_device_ids=true | all-gather | bytes 2304 | tf_op jit(solution)/shard_map/all_gather | solution.py:159
  24.9 17.3 %all_gather.40 = bf16[1024,256]{1,0:T(8,128)(2,1)S(1)} all-gather(bf16[128,256]{1,0:T(8,128)(2,1)S(1)} %copy-done.35), channel_id=1, replica_groups=mesh['rep'=4,'shard'=8] {'shard'}, dimensions={0}, use_global_device_ids=true | all-gather | bytes 589824 | tf_op jit(solution)/shard_map/all_gather | solution.py:157
  74.0 17.6 %all_gather.39 = bf16[1024,256]{1,0:T(8,128)(2,1)S(1)} all-gather(bf16[128,256]{1,0:T(8,128)(2,1)S(1)} %copy-done.36), channel_id=1, replica_groups=mesh['rep'=4,'shard'=8] {'shard'}, dimensions={0}, use_global_device_ids=true | all-gather | bytes 589824 | tf_op jit(solution)/shard_map/all_gather | solution.py:156
  100.2 14.6 %div.136 = bf16[2,512,16,256]{1,0,3,2:T(2,128)(2,1)} reshape(bf16[1024,16,16,16]{0,3,2,1:T(8,128)(2,1)} %multiply_convert_fusion.1) | data formatting | bytes 16777216 | tf_op jit(solution)/shard_map/div | solution.py:26
  114.8 8.6 copy.125
  127.5 9.4 all-gather.2
  140.9 11.8 %pad_maximum_fusion.1 = bf16[2,512,16,273]{1,3,2,0:T(8,128)(2,1)} fusion(bf16[2,512,16,256]{1,3,2,0:T(8,128)(2,1)} %copy.125, bf16[2,512,16,16]{1,3,2,0:T(8,128)(2,1)} %copy.124, bf16[273]{0:T(512)(128)(2,1)S(1)} %pad.12.clone), kind=kLoop, calls=%fused_computation.76 | loop fusion | flops 26836992 | bytes 17859106 | tf_op jit(solution)/shard_map/concatenate | solution.py:22
  156.0 41.7 %while.32 = (s32[]{:T(128)}, f32[4,1024,4,64]{1,3,2,0:T(8,128)}, f32[4,1024,4]{1,2,0:T(4,128)S(1)}, bf16[4,1024,4,64]{1,3,2,0:T(8,128)(2,1)}, bf16[4,1024,4,16]{...) while((s32[]{:T(128)}, f32[4,1024,4,64]{1,3,2,0:T(8,128)}, ...), condition=%wide.region_3.4_spmd.clone, body=%wide.region_1.3_spmd.clone.sunk | while | flops 707784704 | bytes 20764768 | solution.py:199
  235.5 11.5 %fusion.129 = f32[1024,2752]{0,1:T(8,128)} fusion(bf16[1024,2752]{0,1:T(8,128)(2,1)} %all-gather.14.cloned.1.call-done, bf16[1024,1024]{0,1:T(8,128)(2,1)S(1)} %multiply_convert_fusion.6), kind=kOutput, calls=%fused_computation.207 | convolution fusion | flops 5771362304 | bytes 19005440 | tf_op jit(solution)/shard_map/dot_general | solution.py:217
  247.0 26.2 %all-gather.16.cloned.1.call-done = bf16[1024,2752]{0,1:T(8,128)(2,1)} async-done(((bf16[128,2752]{0,1:T(8,128)(2,1)}), bf16[1024,2752]{0,1:T(8,128)(2,1)}) %all-gather.16.cloned.1.call-update) | async-done | bytes 5636112 | tf_op jit(solution)/shard_map/all_gather | solution.py:214
  273.2 11.1 fusion.130
  284.3 48.3 %all-gather.18.cloned.1.call-done = bf16[1024,2752]{0,1:T(8,128)(2,1)} async-done(((bf16[128,2752]{0,1:T(8,128)(2,1)}), bf16[1024,2752]{0,1:T(8,128)(2,1)}) %all-gather.18.cloned.1.call-update) | async-done | bytes 5636112 | tf_op jit(solution)/shard_map/all_gather | solution.py:14
  332.6 20.0 %multiply_convert_fusion.3 = (bf16[1024,2752]{0,1:T(8,128)(2,1)}, bf16[1024,2752]{0,1:T(8,128)(2,1)}, bf16[1024,2752]{0,1:T(8,128)(2,1)}) fusion(f32[1024,2752]{0,1:T(8,128)} %fusion.129, f32[1024,2752]{0,1:T(8,128)} %fusion.130, bf16[1024,1024]{1,0:T(8,128)(2,1)S(1)} %copy-done.25, bf16[1024,2752]{0,1:T(8,128)(2,1)} %all-gather.18.cloned.1.call-done), kind=kOutput, calls=%fused_computation.71 | convolution fusion | flops 5816451072 | bytes 47185920 | tf_op jit(solution)/shard_map/dot_general | solution.py:226
  352.6 11.3 %fusion.128 = f32[1024,1024]{0,1:T(8,128)} fusion(bf16[1024,2752]{0,1:T(8,128)(2,1)} %get-tuple-element.371, bf16[1024,2752]{0,1:T(8,128)(2,1)} %all-gather.14.cloned.1.call-done), kind=kOutput, calls=%fused_computation.206 | convolution fusion | flops 5771362304 | bytes 15466496 | tf_op jit(solution)/shard_map/dot_general | solution.py:33
  363.9 10.8 multiply_reduce_fusion.4
  399.6 152.8 %while.33 = (s32[]{:T(128)}, f32[4,1024,4,16]{1,3,2,0:T(8,128)}, f32[4,1024,4,16]{1,3,2,0:T(8,128)}, f32[4,1024,4,64]{1,3,2,0:T(8,128)}, bf16[4,1024,4,16]{1,3,2...) while((s32[]{:T(128)}, f32[4,1024,4,16]{1,3,2,0:T(8,128)}, ...), condition=%wide.region_8.9_spmd.clone, body=%wide.region_7.8_spmd.clone.sunk | while | flops 1534201856 | bytes 132695256 | solution.py:252
  408.5 10.8 multiply_convert_fusion.10
  446.6 10.8 multiply_convert_fusion.10
  484.7 10.8 multiply_convert_fusion.10
  522.8 10.8 multiply_convert_fusion.10
  569.5 9.2 convolution_convert_fusion.2
  578.7 9.1 copy.164
  594.2 15.3 %copy.165 = f32[2,512,16,273]{1,0,3,2:T(2,128)} copy(f32[2,512,16,273]{1,3,2,0:T(8,128)S(1)} %add_bitcast_fusion.1) | data formatting | bytes 35782656 | tf_op jit(solution)/shard_map/reshape | solution.py:267
  609.5 23.4 %reshape.298 = f32[1024,16,273]{0,2,1:T(8,128)} reshape(f32[2,512,16,273]{1,0,3,2:T(2,128)} %copy.165) | data formatting | bytes 35782656 | tf_op jit(solution)/shard_map/reshape | solution.py:267
  643.0 10.5 fusion.63
  670.2 12.0 %multiply_reduce_fusion.3 = (f32[1024,16,16]{0,2,1:T(8,128)S(1)}, f32[1024,16,16]{0,2,1:T(8,128)S(1)}) fusion(f32[1024,16,16,16]{0,3,2,1:T(8,128)S(1)} %bitcast.295, f32[1024,16,16]{0,2,1:T(8,128)S(1)} %copy-done.8, f32[1024,16,273]{0,2,1:T(8,128)} %reshape.298), kind=kLoop, calls=%fused_computation.64 | loop fusion | flops 20447232 | bytes 37748736 | tf_op jit(solution)/shard_map/transpose(jvp())/reduce_sum | solution.py:20
  682.3 18.4 %convolution_convert_fusion = bf16[1024,5504]{1,0:T(8,128)(2,1)} fusion(bf16[1024,1024]{0,1:T(8,128)(2,1)} %copy-done.27, bf16[1024,2752]{0,1:T(8,128)(2,1)} %get-tuple-element.370, bf16[1024,2752]{0,1:T(8,128)(2,1)} %get-tuple-element.371), kind=kOutput, calls=%fused_computation.67 | convolution fusion | flops 11570905088 | bytes 24641536 | tf_op jit(solution)/shard_map/dot_general | solution.py:39
  720.1 12.1 %multiply_reduce_fusion.1 = (f32[1024,16,16]{0,2,1:T(8,128)S(1)}, f32[1024,16,16]{0,2,1:T(8,128)S(1)}) fusion(f32[1024,16,16,16]{0,3,2,1:T(8,128)} %bitcast.296, f32[1024,16,16]{0,2,1:T(8,128)S(1)} %copy-done.11, f32[1024,16,273]{0,2,1:T(8,128)S(1)} %add_bitcast_fusion), kind=kLoop, calls=%fused_computation.62 | loop fusion | flops 20447232 | bytes 37748736 | tf_op jit(solution)/shard_map/transpose(jvp())/reduce_sum | solution.py:20
  749.1 41.9 %concatenate.35 = bf16[1024,10818]{1,0:T(8,128)(2,1)} concatenate(bf16[1024,1536]{1,0:T(8,128)(2,1)} %convolution_convert_fusion.3, bf16[1024,1024]{1,0:T(8,128)(2,1)} %copy.143, bf16[1024,5504]{1,0:T(8,128)(2,1)} %convolution_convert_fusion, bf16[1024,2752]{1,0:T(8,128)(2,1)} %copy.144, bf16[1024,1]{1,0:T(8,128)(2,1)S(1)} %broadcast_in_dim.128, ...), dimensions={1} | concatenate | bytes 44310528 | tf_op jit(solution)/shard_map/concatenate | solution.py:326
  791.1 218.2 %reduce-scatter.5.cloned.1.call-done = bf16[128,10818]{1,0:T(8,128)(2,1)} async-done(((bf16[1024,10818]{1,0:T(8,128)(2,1)}), bf16[128,10818]{1,0:T(8,128)(2,1)}) %reduce-scatter.5.cloned.1.call-update) | async-done | bytes 2769424 | tf_op jit(solution)/shard_map/reduce_scatter | solution.py:325
  1009.3 11.7 %add_convert_fusion = bf16[1024,1024]{0,1:T(8,128)(2,1)} fusion(f32[1024,1024]{0,1:T(8,128)} %copy-done.12, bf16[1024,2752]{0,1:T(8,128)(2,1)} %get-tuple-element.372, bf16[1024,2752]{0,1:T(8,128)(2,1)} %all-gather.18.cloned.1.call-done), kind=kOutput, calls=%fused_computation.111 | convolution fusion | flops 5773459456 | bytes 17563648 | tf_op jit(solution)/shard_map/dot_general | solution.py:33
  1037.0 55.2 %all-reduce.2.cloned.1.call-done = bf16[128,10818]{1,0:T(8,128)(2,1)} async-done(((bf16[128,10818]{1,0:T(8,128)(2,1)}), bf16[128,10818]{1,0:T(8,128)(2,1)}) %all-reduce.2.cloned.1.call-update) | async-done | bytes 2769424 | tf_op jit(solution)/shard_map/psum | solution.py:341
  (321 shorter events, 383.0 us)
Async XLA Ops:
  7.2 47.4 %all-gather.10.cloned.1.call-start = ((), (), s32[]{:S(2)}) async-start(), calls=%async_computation.2 | async-start | bytes 2359296 | tf_op jit(solution)/shard_map/all_gather | solution.py:158
  7.9 190.4 %all-gather.20.cloned.1.call-start = ((), (), s32[]{:S(2)}) async-start(), calls=%async_computation.10 | async-start | bytes 5806080 | tf_op jit(solution)/shard_map/all_gather | solution.py:180
  10.8 216.3 %copy-start.5 = (bf16[1024,1024]{0,1:T(8,128)(2,1)}, bf16[1024,1024]{0,1:T(8,128)(2,1)S(1)}, u32[]{:S(2)}) copy-start(bf16[1024,1024]{0,1:T(8,128)(2,1)S(1)} %copy.120) | copy-start | bytes 6291460
  24.3 67.3 %copy-start.40 = (f32[8,1,128]{2,1,0:T(1,128)}, f32[8,1,128]{2,1,0:T(1,128)S(1)}, u32[]{:S(2)}) copy-start(f32[8,1,128]{2,1,0:T(1,128)S(1)} %convert_element_type.208) | copy-start | bytes 12292
  24.4 116.6 %copy-start.44 = (bf16[273]{0:T(512)(128)(2,1)}, bf16[273]{0:T(512)(128)(2,1)S(1)}, u32[]{:S(2)}) copy-start(bf16[273]{0:T(512)(128)(2,1)S(1)} %pad.12.clone) | copy-start | bytes 1642
  24.9 66.8 %copy-start.42 = (f32[1024]{0:T(1024)}, f32[1024]{0:T(1024)S(1)}, u32[]{:S(2)}) copy-start(f32[1024]{0:T(1024)S(1)} %add_rsqrt_fusion.1) | copy-start | bytes 12292
  65.7 161.5 %all-gather.12.cloned.1.call-start = ((), (), s32[]{:S(2)}) async-start(), calls=%async_computation.3 | async-start | bytes 2359296 | tf_op jit(solution)/shard_map/all_gather | solution.py:14
  66.4 167.8 %all-gather.14.cloned.1.call-start = ((), (), s32[]{:S(2)}) async-start(), calls=%async_computation.4 | async-start | bytes 6340608 | tf_op jit(solution)/shard_map/all_gather | solution.py:213
  67.0 206.3 %all-gather.16.cloned.1.call-start = ((), (), s32[]{:S(2)}) async-start(), calls=%async_computation.5 | async-start | bytes 6340608 | tf_op jit(solution)/shard_map/all_gather | solution.py:214
  67.6 265.1 %all-gather.18.cloned.1.call-start = ((), (), s32[]{:S(2)}) async-start(), calls=%async_computation.6 | async-start | bytes 6340608 | tf_op jit(solution)/shard_map/all_gather | solution.py:14
  68.1 632.5 %reduce-scatter.3.cloned.1.call-start = ((), (), s32[]{:S(2)}) async-start(), calls=%async_computation.7 | async-start | bytes 7188480 | tf_op jit(solution)/shard_map/reduce_scatter | solution.py:276
  73.3 125.0 %copy-start.51 = (pred[1,8]{1,0:T(4,128)(4,1)}, pred[1,8]{1,0:T(4,128)(4,1)S(1)}, u32[]{:S(2)}) copy-start(pred[1,8]{1,0:T(4,128)(4,1)S(1)} %get-tuple-element.366) | copy-start | bytes 28
  153.4 45.0 %copy-start.47 = (pred[1,8]{1,0:T(4,128)(4,1)}, pred[1,8]{1,0:T(4,128)(4,1)S(1)}, u32[]{:S(2)}) copy-start(pred[1,8]{1,0:T(4,128)(4,1)S(1)} %get-tuple-element.384) | copy-start | bytes 28
  153.4 45.0 %copy-start.49 = (pred[1,8]{1,0:T(4,128)(4,1)}, pred[1,8]{1,0:T(4,128)(4,1)S(1)}, u32[]{:S(2)}) copy-start(pred[1,8]{1,0:T(4,128)(4,1)S(1)} %get-tuple-element.385) | copy-start | bytes 28
  247.0 85.6 %copy-start.25 = (bf16[1024,1024]{1,0:T(8,128)(2,1)S(1)}, bf16[1024,1024]{1,0:T(8,128)(2,1)}, u32[]{:S(2)}) copy-start(bf16[1024,1024]{1,0:T(8,128)(2,1)} %param.29) | copy-start | bytes 6291460
  399.6 152.8 %copy-start.30 = (f32[2,16,1,512]{3,2,1,0:T(1,128)S(1)}, f32[2,16,1,512]{3,2,1,0:T(1,128)}, u32[]{:S(2)}) copy-start(f32[2,16,1,512]{3,2,1,0:T(1,128)} %copy-done.29) | copy-start | bytes 196612
  399.6 152.8 %copy-start.33 = (f32[2,512,16]{1,0,2:T(2,128)S(1)}, f32[2,512,16]{1,0,2:T(2,128)}, u32[]{:S(2)}) copy-start(f32[2,512,16]{1,0,2:T(2,128)} %reshape.269) | copy-start | bytes 196612
  399.6 152.8 %copy-start.34 = (f32[2,512,16]{1,0,2:T(2,128)S(1)}, f32[2,512,16]{1,0,2:T(2,128)}, u32[]{:S(2)}) copy-start(f32[2,512,16]{1,0,2:T(2,128)} %neg.17) | copy-start | bytes 196612
  408.5 23.3 %slice-start = ((s8[16777216]{0:T(1024)(128)(4,1)}), s8[4194304]{0:T(1024)(128)(4,1)S(1)}, s32[]{:S(2)}) async-start(s8[16777216]{0:T(1024)(128)(4,1)} %bitcast.291), calls=%async_computation.11 | async-start | bytes 8388608 | tf_op jit(solution)/shard_map/while
  408.5 23.3 %slice-start.1 = ((s8[16777216]{0:T(1024)(128)(4,1)}), s8[4194304]{0:T(1024)(128)(4,1)S(1)}, s32[]{:S(2)}) async-start(s8[16777216]{0:T(1024)(128)(4,1)} %bitcast.291), calls=%async_computation.12 | async-start | bytes 8388608 | tf_op jit(solution)/shard_map/while
  446.6 23.3 %slice-start = ((s8[16777216]{0:T(1024)(128)(4,1)}), s8[4194304]{0:T(1024)(128)(4,1)S(1)}, s32[]{:S(2)}) async-start(s8[16777216]{0:T(1024)(128)(4,1)} %bitcast.291), calls=%async_computation.11 | async-start | bytes 8388608 | tf_op jit(solution)/shard_map/while
  446.6 23.3 %slice-start.1 = ((s8[16777216]{0:T(1024)(128)(4,1)}), s8[4194304]{0:T(1024)(128)(4,1)S(1)}, s32[]{:S(2)}) async-start(s8[16777216]{0:T(1024)(128)(4,1)} %bitcast.291), calls=%async_computation.12 | async-start | bytes 8388608 | tf_op jit(solution)/shard_map/while
  446.6 23.3 %slice-start.2 = ((s8[16777216]{0:T(1024)(128)(4,1)}), s8[4194304]{0:T(1024)(128)(4,1)S(1)}, s32[]{:S(2)}) async-start(s8[16777216]{0:T(1024)(128)(4,1)} %bitcast.291), calls=%async_computation.13 | async-start | bytes 8388608 | tf_op jit(solution)/shard_map/while
  484.7 23.3 %slice-start = ((s8[16777216]{0:T(1024)(128)(4,1)}), s8[4194304]{0:T(1024)(128)(4,1)S(1)}, s32[]{:S(2)}) async-start(s8[16777216]{0:T(1024)(128)(4,1)} %bitcast.291), calls=%async_computation.11 | async-start | bytes 8388608 | tf_op jit(solution)/shard_map/while
  484.7 23.3 %slice-start.1 = ((s8[16777216]{0:T(1024)(128)(4,1)}), s8[4194304]{0:T(1024)(128)(4,1)S(1)}, s32[]{:S(2)}) async-start(s8[16777216]{0:T(1024)(128)(4,1)} %bitcast.291), calls=%async_computation.12 | async-start | bytes 8388608 | tf_op jit(solution)/shard_map/while
  484.7 23.3 %slice-start.2 = ((s8[16777216]{0:T(1024)(128)(4,1)}), s8[4194304]{0:T(1024)(128)(4,1)S(1)}, s32[]{:S(2)}) async-start(s8[16777216]{0:T(1024)(128)(4,1)} %bitcast.291), calls=%async_computation.13 | async-start | bytes 8388608 | tf_op jit(solution)/shard_map/while
  522.8 23.3 %slice-start = ((s8[16777216]{0:T(1024)(128)(4,1)}), s8[4194304]{0:T(1024)(128)(4,1)S(1)}, s32[]{:S(2)}) async-start(s8[16777216]{0:T(1024)(128)(4,1)} %bitcast.291), calls=%async_computation.11 | async-start | bytes 8388608 | tf_op jit(solution)/shard_map/while
  522.8 23.3 %slice-start.1 = ((s8[16777216]{0:T(1024)(128)(4,1)}), s8[4194304]{0:T(1024)(128)(4,1)S(1)}, s32[]{:S(2)}) async-start(s8[16777216]{0:T(1024)(128)(4,1)} %bitcast.291), calls=%async_computation.12 | async-start | bytes 8388608 | tf_op jit(solution)/shard_map/while
  522.8 23.3 %slice-start.2 = ((s8[16777216]{0:T(1024)(128)(4,1)}), s8[4194304]{0:T(1024)(128)(4,1)S(1)}, s32[]{:S(2)}) async-start(s8[16777216]{0:T(1024)(128)(4,1)} %bitcast.291), calls=%async_computation.13 | async-start | bytes 8388608 | tf_op jit(solution)/shard_map/while
  587.8 421.5 %reduce-scatter.5.cloned.1.call-start = ((), (), s32[]{:S(2)}) async-start(), calls=%async_computation.8 | async-start | bytes 25067520 | tf_op jit(solution)/shard_map/reduce_scatter | solution.py:325
  609.5 23.4 %copy-start.22 = (bf16[1024,1024]{0,1:T(8,128)(2,1)S(1)}, bf16[1024,1024]{0,1:T(8,128)(2,1)}, u32[]{:S(2)}) copy-start(bf16[1024,1024]{0,1:T(8,128)(2,1)} %fusion.75) | copy-start | bytes 6291460
  791.0 301.1 %all-reduce.2.cloned.1.call-start = ((), (), s32[]{:S(2)}) async-start(), calls=%async_computation.9 | async-start | bytes 5570560 | tf_op jit(solution)/shard_map/psum | solution.py:341
  (56 other events, 379.5 us)
Sparse Core Ops, SparseCore 0:
  9.6 36.0 all-gather.9
  65.8 57.8 all-gather.19
  125.3 27.8 all-gather.11
  154.7 59.1 all-gather.13
  215.3 57.9 all-gather.15
  274.7 57.9 all-gather.17
  588.0 69.0 reduce-scatter.2
  791.2 218.1 reduce-scatter.4
  1012.5 79.6 all-reduce.1
where the time goes:
time: 1130 us; the launch traced here: 1110 us
  matrix products  391 us (35%)
  waiting for transfers between devices  351 us (31%)
  local copies, waits for them, and re-layouts  204 us (18%)
  other arithmetic  90.3 us (8%)
  blocking collectives  57.8 us (5%)
  between operations  19.1 us (2%)
    reduce_scatter x1, waiting for transfers between devices, local(): lax.psum_scatter(jnp.concatenate([contract_first(pick(hidden_one), grad_q...  218 us
    dot_general x8, matrix products, kernel_of(): jnp.einsum('thf,uhf->htu', queries, key_heads, preferred_element_type=jnp...  57.4 us
    psum x1, waiting for transfers between devices, local(): own_grads = lax.psum(group_share, 'rep').astype(jnp.float32)  55.2 us
    all_gather x2, waiting for transfers between devices, on_whole(): whole = lax.all_gather(value, axis, axis=dim, tiled=True)  48.3 us
    dot_general x7, matrix products, contract_last(): lax.dot_general(left, right, (((1,), (1,)), ((), ())), preferred_element_...  44.6 us
    dot_general x4, matrix products, local_backward(): jnp.einsum('the,uhe->htu', grad_num, value_heads, preferred_element_type=...  43.1 us
    concatenate x1, local copies, waits for them, and re-layouts, local(): jnp.concatenate([contract_first(pick(hidden_one), grad_qkv), contract_fir...  41.9 us
    dot_general x4, matrix products, contract_first(): lax.dot_general(left, right, (((0,), (0,)), ((), ())), preferred_element_...  40.9 us
  transfers between devices with their start and end apart: 9, of which 4 were waited for; matrix products, arithmetic and copies ran while one was open for 28% of the time, Pallas kernels for 0%

commit v1 on v0

--- a/solution.py
+++ b/solution.py
@@ -338,7 +338,7 @@
         scatter_dimension=0,
         tiled=True,
     )
-    own_grads = lax.psum(group_share, "rep").astype(jnp.float32)
+    own_grads = jnp.sum(lax.all_gather(group_share, "rep"), axis=0).astype(jnp.float32)
     edge_two = qk_width + qk_width
     edge_three = edge_two + value_width
     edge_four = edge_three + value_width

time: 1130 us -> 1160 us (1.027)
  waiting for transfers between devices: 351 us -> 379 us
    all_gather x0 -> x1, waiting for transfers between devices: none -> 83.1 us  [local(): lax.all_gather(group_share, 'rep')]
    psum x1 -> x0, waiting for transfers between devices: 55.2 us -> none  [local(): own_grads = lax.psum(group_share, 'rep').astype(jnp.float32)]
  transfers between devices with their start and end apart: 9 -> 9, of which waited for: 4 -> 4; matrix products, arithmetic and copies ran while one was open for 28% -> 27% of each run, Pallas kernels for 0% -> 0%
where the time goes in v1:
time: 1160 us; the launch traced here: 1150 us
  matrix products  391 us (34%)
  waiting for transfers between devices  379 us (33%)
  local copies, waits for them, and re-layouts  202 us (17%)
  other arithmetic  98.7 us (9%)
  blocking collectives  57.8 us (5%)
  between operations  19.1 us (2%)
    reduce_scatter x1, waiting for transfers between devices, local(): lax.psum_scatter(jnp.concatenate([contract_first(pick(hidden_one), grad_q...  218 us
    all_gather x1, waiting for transfers between devices, local(): lax.all_gather(group_share, 'rep')  83.1 us
    dot_general x8, matrix products, kernel_of(): jnp.einsum('thf,uhf->htu', queries, key_heads, preferred_element_type=jnp...  57.4 us
    all_gather x2, waiting for transfers between devices, on_whole(): whole = lax.all_gather(value, axis, axis=dim, tiled=True)  48.3 us
    dot_general x7, matrix products, contract_last(): lax.dot_general(left, right, (((1,), (1,)), ((), ())), preferred_element_...  44.6 us
    dot_general x4, matrix products, local_backward(): jnp.einsum('the,uhe->htu', grad_num, value_heads, preferred_element_type=...  43.1 us
    concatenate x1, local copies, waits for them, and re-layouts, local(): jnp.concatenate([contract_first(pick(hidden_one), grad_qkv), contract_fir...  41.9 us
    dot_general x4, matrix products, contract_first(): lax.dot_general(left, right, (((0,), (0,)), ((), ())), preferred_element_...  40.9 us
  transfers between devices with their start and end apart: 9, of which 4 were waited for; matrix products, arithmetic and copies ran while one was open for 27% of the time, Pallas kernels for 0%

profile of v1, /device:TPU:0, one launch (start us, length us, event | category | flops | bytes accessed | tf_op | source)
XLA Modules:
  0.0 1149.1 jit_solution(10273940848879646815)
XLA Ops:
  10.9 13.5 %all-gather.1 = bf16[8,1,128]{2,1,0:T(2,128)(2,1)S(1)} all-gather(bf16[1,1,128]{2,1,0:T(2,128)(2,1)S(1)} %bitcast.341), channel_id=1, replica_groups=mesh['rep'=4,'shard'=8] {'shard'}, dimensions={0}, use_global_device_ids=true | all-gather | bytes 2304 | tf_op jit(solution)/shard_map/all_gather | solution.py:159
  24.9 17.3 %all_gather.46 = bf16[1024,256]{1,0:T(8,128)(2,1)S(1)} all-gather(bf16[128,256]{1,0:T(8,128)(2,1)S(1)} %copy-done.35), channel_id=1, replica_groups=mesh['rep'=4,'shard'=8] {'shard'}, dimensions={0}, use_global_device_ids=true | all-gather | bytes 589824 | tf_op jit(solution)/shard_map/all_gather | solution.py:157
  74.0 17.6 %all_gather.45 = bf16[1024,256]{1,0:T(8,128)(2,1)S(1)} all-gather(bf16[128,256]{1,0:T(8,128)(2,1)S(1)} %copy-done.36), channel_id=1, replica_groups=mesh['rep'=4,'shard'=8] {'shard'}, dimensions={0}, use_global_device_ids=true | all-gather | bytes 589824 | tf_op jit(solution)/shard_map/all_gather | solution.py:156
  100.2 14.6 %div.136 = bf16[2,512,16,256]{1,0,3,2:T(2,128)(2,1)} reshape(bf16[1024,16,16,16]{0,3,2,1:T(8,128)(2,1)} %multiply_convert_fusion.1) | data formatting | bytes 16777216 | tf_op jit(solution)/shard_map/div | solution.py:26
  114.8 8.6 copy.161
  127.5 9.4 all-gather.3
  140.9 11.8 %pad_maximum_fusion.1 = bf16[2,512,16,273]{1,3,2,0:T(8,128)(2,1)} fusion(bf16[2,512,16,256]{1,3,2,0:T(8,128)(2,1)} %copy.161, bf16[2,512,16,16]{1,3,2,0:T(8,128)(2,1)} %copy.160, bf16[273]{0:T(512)(128)(2,1)S(1)} %pad.12.clone), kind=kLoop, calls=%fused_computation.76 | loop fusion | flops 26836992 | bytes 17859106 | tf_op jit(solution)/shard_map/concatenate | solution.py:22
  156.0 41.7 %while.32 = (s32[]{:T(128)}, f32[4,1024,4,64]{1,3,2,0:T(8,128)}, f32[4,1024,4]{1,2,0:T(4,128)S(1)}, bf16[4,1024,4,64]{1,3,2,0:T(8,128)(2,1)}, bf16[4,1024,4,16]{...) while((s32[]{:T(128)}, f32[4,1024,4,64]{1,3,2,0:T(8,128)}, ...), condition=%wide.region_3.4_spmd.clone, body=%wide.region_1.3_spmd.clone.sunk | while | flops 707784704 | bytes 20764768 | solution.py:199
  235.5 11.5 fusion.129
  247.0 26.2 %all-gather.18.cloned.1.call-done = bf16[1024,2752]{0,1:T(8,128)(2,1)} async-done(((bf16[128,2752]{0,1:T(8,128)(2,1)}), bf16[1024,2752]{0,1:T(8,128)(2,1)}) %all-gather.18.cloned.1.call-update) | async-done | bytes 5636112 | tf_op jit(solution)/shard_map/all_gather | solution.py:214
  273.2 11.1 fusion.130
  284.3 48.3 %all-gather.20.cloned.1.call-done = bf16[1024,2752]{0,1:T(8,128)(2,1)} async-done(((bf16[128,2752]{0,1:T(8,128)(2,1)}), bf16[1024,2752]{0,1:T(8,128)(2,1)}) %all-gather.20.cloned.1.call-update) | async-done | bytes 5636112 | tf_op jit(solution)/shard_map/all_gather | solution.py:14
  332.6 20.0 %multiply_convert_fusion.3 = (bf16[1024,2752]{0,1:T(8,128)(2,1)}, bf16[1024,2752]{0,1:T(8,128)(2,1)}, bf16[1024,2752]{0,1:T(8,128)(2,1)}) fusion(f32[1024,2752]{0,1:T(8,128)} %fusion.129, f32[1024,2752]{0,1:T(8,128)} %fusion.130, bf16[1024,1024]{1,0:T(8,128)(2,1)S(1)} %copy-done.25, bf16[1024,2752]{0,1:T(8,128)(2,1)} %all-gather.20.cloned.1.call-done), kind=kOutput, calls=%fused_computation.71 | convolution fusion | flops 5816451072 | bytes 47185920 | tf_op jit(solution)/shard_map/dot_general | solution.py:226
  352.6 11.3 fusion.128
  363.9 10.8 multiply_reduce_fusion.4
  399.6 152.8 %while.33 = (s32[]{:T(128)}, f32[4,1024,4,16]{1,3,2,0:T(8,128)}, f32[4,1024,4,16]{1,3,2,0:T(8,128)}, f32[4,1024,4,64]{1,3,2,0:T(8,128)}, bf16[4,1024,4,16]{1,3,2...) while((s32[]{:T(128)}, f32[4,1024,4,16]{1,3,2,0:T(8,128)}, ...), condition=%wide.region_8.9_spmd.clone, body=%wide.region_7.8_spmd.clone.sunk | while | flops 1534201856 | bytes 132695256 | solution.py:252
  408.5 10.8 multiply_convert_fusion.10
  446.6 10.8 multiply_convert_fusion.10
  484.7 10.8 multiply_convert_fusion.10
  522.8 10.8 multiply_convert_fusion.10
  569.5 9.2 convolution_convert_fusion.2
  578.7 9.1 copy.200
  594.2 15.3 %copy.201 = f32[2,512,16,273]{1,0,3,2:T(2,128)} copy(f32[2,512,16,273]{1,3,2,0:T(8,128)S(1)} %add_bitcast_fusion.1) | data formatting | bytes 35782656 | tf_op jit(solution)/shard_map/reshape | solution.py:267
  609.5 23.4 %reshape.299 = f32[1024,16,273]{0,2,1:T(8,128)} reshape(f32[2,512,16,273]{1,0,3,2:T(2,128)} %copy.201) | data formatting | bytes 35782656 | tf_op jit(solution)/shard_map/reshape | solution.py:267
  643.0 10.5 fusion.63
  670.2 12.0 %multiply_reduce_fusion.3 = (f32[1024,16,16]{0,2,1:T(8,128)S(1)}, f32[1024,16,16]{0,2,1:T(8,128)S(1)}) fusion(f32[1024,16,16,16]{0,3,2,1:T(8,128)S(1)} %bitcast.296, f32[1024,16,16]{0,2,1:T(8,128)S(1)} %copy-done.8, f32[1024,16,273]{0,2,1:T(8,128)} %reshape.299), kind=kLoop, calls=%fused_computation.64 | loop fusion | flops 20447232 | bytes 37748736 | tf_op jit(solution)/shard_map/transpose(jvp())/reduce_sum | solution.py:20
  682.3 18.4 %convolution_convert_fusion = bf16[1024,5504]{1,0:T(8,128)(2,1)} fusion(bf16[1024,1024]{0,1:T(8,128)(2,1)} %copy-done.27, bf16[1024,2752]{0,1:T(8,128)(2,1)} %get-tuple-element.381, bf16[1024,2752]{0,1:T(8,128)(2,1)} %get-tuple-element.382), kind=kOutput, calls=%fused_computation.67 | convolution fusion | flops 11570905088 | bytes 24641536 | tf_op jit(solution)/shard_map/dot_general | solution.py:39
  720.1 12.1 %multiply_reduce_fusion.1 = (f32[1024,16,16]{0,2,1:T(8,128)S(1)}, f32[1024,16,16]{0,2,1:T(8,128)S(1)}) fusion(f32[1024,16,16,16]{0,3,2,1:T(8,128)} %bitcast.297, f32[1024,16,16]{0,2,1:T(8,128)S(1)} %copy-done.10, f32[1024,16,273]{0,2,1:T(8,128)S(1)} %add_bitcast_fusion), kind=kLoop, calls=%fused_computation.62 | loop fusion | flops 20447232 | bytes 37748736 | tf_op jit(solution)/shard_map/transpose(jvp())/reduce_sum | solution.py:20
  749.1 41.9 %concatenate.35 = bf16[1024,10818]{1,0:T(8,128)(2,1)} concatenate(bf16[1024,1536]{1,0:T(8,128)(2,1)} %convolution_convert_fusion.3, bf16[1024,1024]{1,0:T(8,128)(2,1)} %copy.179, bf16[1024,5504]{1,0:T(8,128)(2,1)} %convolution_convert_fusion, bf16[1024,2752]{1,0:T(8,128)(2,1)} %copy.180, bf16[1024,1]{1,0:T(8,128)(2,1)S(1)} %broadcast_in_dim.128, ...), dimensions={1} | concatenate | bytes 44310528 | tf_op jit(solution)/shard_map/concatenate | solution.py:326
  791.1 218.2 %reduce-scatter.5.cloned.1.call-done = bf16[128,10818]{1,0:T(8,128)(2,1)} async-done(((bf16[1024,10818]{1,0:T(8,128)(2,1)}), bf16[128,10818]{1,0:T(8,128)(2,1)}) %reduce-scatter.5.cloned.1.call-update) | async-done | bytes 2769424 | tf_op jit(solution)/shard_map/reduce_scatter | solution.py:325
  1009.3 11.7 %add_convert_fusion = bf16[1024,1024]{0,1:T(8,128)(2,1)} fusion(f32[1024,1024]{0,1:T(8,128)} %copy-done.11, bf16[1024,2752]{0,1:T(8,128)(2,1)} %get-tuple-element.383, bf16[1024,2752]{0,1:T(8,128)(2,1)} %all-gather.20.cloned.1.call-done), kind=kOutput, calls=%fused_computation.111 | convolution fusion | flops 5773459456 | bytes 17563648 | tf_op jit(solution)/shard_map/dot_general | solution.py:33
  1037.0 83.1 %all-gather.22.cloned.1.call-done = bf16[512,10818]{1,0:T(8,128)(2,1)} async-done(((bf16[128,10818]{1,0:T(8,128)(2,1)}), bf16[512,10818]{1,0:T(8,128)(2,1)}) %all-gather.22.cloned.1.call-update) | async-done | bytes 11077648 | tf_op jit(solution)/shard_map/all_gather | solution.py:341
  (322 shorter events, 389.5 us)
Async XLA Ops:
  7.2 47.4 %all-gather.12.cloned.1.call-start = ((), (), s32[]{:S(2)}) async-start(), calls=%async_computation.2 | async-start | bytes 2359296 | tf_op jit(solution)/shard_map/all_gather | solution.py:158
  7.9 190.4 %all-gather.24.cloned.1.call-start = ((), (), s32[]{:S(2)}) async-start(), calls=%async_computation.10 | async-start | bytes 5806080 | tf_op jit(solution)/shard_map/all_gather | solution.py:180
  10.8 216.3 %copy-start.5 = (bf16[1024,1024]{0,1:T(8,128)(2,1)}, bf16[1024,1024]{0,1:T(8,128)(2,1)S(1)}, u32[]{:S(2)}) copy-start(bf16[1024,1024]{0,1:T(8,128)(2,1)S(1)} %copy.156) | copy-start | bytes 6291460
  24.3 67.3 %copy-start.40 = (f32[8,1,128]{2,1,0:T(1,128)}, f32[8,1,128]{2,1,0:T(1,128)S(1)}, u32[]{:S(2)}) copy-start(f32[8,1,128]{2,1,0:T(1,128)S(1)} %convert_element_type.210) | copy-start | bytes 12292
  24.4 116.6 %copy-start.44 = (bf16[273]{0:T(512)(128)(2,1)}, bf16[273]{0:T(512)(128)(2,1)S(1)}, u32[]{:S(2)}) copy-start(bf16[273]{0:T(512)(128)(2,1)S(1)} %pad.12.clone) | copy-start | bytes 1642
  24.9 66.8 %copy-start.42 = (f32[1024]{0:T(1024)}, f32[1024]{0:T(1024)S(1)}, u32[]{:S(2)}) copy-start(f32[1024]{0:T(1024)S(1)} %add_rsqrt_fusion.1) | copy-start | bytes 12292
  65.7 161.5 %all-gather.14.cloned.1.call-start = ((), (), s32[]{:S(2)}) async-start(), calls=%async_computation.3 | async-start | bytes 2359296 | tf_op jit(solution)/shard_map/all_gather | solution.py:14
  66.4 167.8 %all-gather.16.cloned.1.call-start = ((), (), s32[]{:S(2)}) async-start(), calls=%async_computation.4 | async-start | bytes 6340608 | tf_op jit(solution)/shard_map/all_gather | solution.py:213
  67.0 206.3 %all-gather.18.cloned.1.call-start = ((), (), s32[]{:S(2)}) async-start(), calls=%async_computation.5 | async-start | bytes 6340608 | tf_op jit(solution)/shard_map/all_gather | solution.py:214
  67.6 265.1 %all-gather.20.cloned.1.call-start = ((), (), s32[]{:S(2)}) async-start(), calls=%async_computation.6 | async-start | bytes 6340608 | tf_op jit(solution)/shard_map/all_gather | solution.py:14
  68.1 632.5 %reduce-scatter.3.cloned.1.call-start = ((), (), s32[]{:S(2)}) async-start(), calls=%async_computation.7 | async-start | bytes 7188480 | tf_op jit(solution)/shard_map/reduce_scatter | solution.py:276
  73.3 125.0 %copy-start.51 = (pred[1,8]{1,0:T(4,128)(4,1)}, pred[1,8]{1,0:T(4,128)(4,1)S(1)}, u32[]{:S(2)}) copy-start(pred[1,8]{1,0:T(4,128)(4,1)S(1)} %get-tuple-element.377) | copy-start | bytes 28
  153.4 45.0 %copy-start.47 = (pred[1,8]{1,0:T(4,128)(4,1)}, pred[1,8]{1,0:T(4,128)(4,1)S(1)}, u32[]{:S(2)}) copy-start(pred[1,8]{1,0:T(4,128)(4,1)S(1)} %get-tuple-element.395) | copy-start | bytes 28
  153.4 45.0 %copy-start.49 = (pred[1,8]{1,0:T(4,128)(4,1)}, pred[1,8]{1,0:T(4,128)(4,1)S(1)}, u32[]{:S(2)}) copy-start(pred[1,8]{1,0:T(4,128)(4,1)S(1)} %get-tuple-element.396) | copy-start | bytes 28
  247.0 85.6 %copy-start.25 = (bf16[1024,1024]{1,0:T(8,128)(2,1)S(1)}, bf16[1024,1024]{1,0:T(8,128)(2,1)}, u32[]{:S(2)}) copy-start(bf16[1024,1024]{1,0:T(8,128)(2,1)} %param.29) | copy-start | bytes 6291460
  399.6 152.8 %copy-start.30 = (f32[2,16,1,512]{3,2,1,0:T(1,128)S(1)}, f32[2,16,1,512]{3,2,1,0:T(1,128)}, u32[]{:S(2)}) copy-start(f32[2,16,1,512]{3,2,1,0:T(1,128)} %copy-done.29) | copy-start | bytes 196612
  399.6 152.8 %copy-start.33 = (f32[2,512,16]{1,0,2:T(2,128)S(1)}, f32[2,512,16]{1,0,2:T(2,128)}, u32[]{:S(2)}) copy-start(f32[2,512,16]{1,0,2:T(2,128)} %reshape.269) | copy-start | bytes 196612
  399.6 152.8 %copy-start.34 = (f32[2,512,16]{1,0,2:T(2,128)S(1)}, f32[2,512,16]{1,0,2:T(2,128)}, u32[]{:S(2)}) copy-start(f32[2,512,16]{1,0,2:T(2,128)} %neg.17) | copy-start | bytes 196612
  408.5 23.3 %slice-start = ((s8[16777216]{0:T(1024)(128)(4,1)}), s8[4194304]{0:T(1024)(128)(4,1)S(1)}, s32[]{:S(2)}) async-start(s8[16777216]{0:T(1024)(128)(4,1)} %bitcast.292), calls=%async_computation.11 | async-start | bytes 8388608 | tf_op jit(solution)/shard_map/while
  408.5 23.3 %slice-start.1 = ((s8[16777216]{0:T(1024)(128)(4,1)}), s8[4194304]{0:T(1024)(128)(4,1)S(1)}, s32[]{:S(2)}) async-start(s8[16777216]{0:T(1024)(128)(4,1)} %bitcast.292), calls=%async_computation.12 | async-start | bytes 8388608 | tf_op jit(solution)/shard_map/while
  446.6 23.3 %slice-start = ((s8[16777216]{0:T(1024)(128)(4,1)}), s8[4194304]{0:T(1024)(128)(4,1)S(1)}, s32[]{:S(2)}) async-start(s8[16777216]{0:T(1024)(128)(4,1)} %bitcast.292), calls=%async_computation.11 | async-start | bytes 8388608 | tf_op jit(solution)/shard_map/while
  446.6 23.3 %slice-start.1 = ((s8[16777216]{0:T(1024)(128)(4,1)}), s8[4194304]{0:T(1024)(128)(4,1)S(1)}, s32[]{:S(2)}) async-start(s8[16777216]{0:T(1024)(128)(4,1)} %bitcast.292), calls=%async_computation.12 | async-start | bytes 8388608 | tf_op jit(solution)/shard_map/while
  446.6 23.3 %slice-start.2 = ((s8[16777216]{0:T(1024)(128)(4,1)}), s8[4194304]{0:T(1024)(128)(4,1)S(1)}, s32[]{:S(2)}) async-start(s8[16777216]{0:T(1024)(128)(4,1)} %bitcast.292), calls=%async_computation.13 | async-start | bytes 8388608 | tf_op jit(solution)/shard_map/while
  484.7 23.3 %slice-start = ((s8[16777216]{0:T(1024)(128)(4,1)}), s8[4194304]{0:T(1024)(128)(4,1)S(1)}, s32[]{:S(2)}) async-start(s8[16777216]{0:T(1024)(128)(4,1)} %bitcast.292), calls=%async_computation.11 | async-start | bytes 8388608 | tf_op jit(solution)/shard_map/while
  484.7 23.3 %slice-start.1 = ((s8[16777216]{0:T(1024)(128)(4,1)}), s8[4194304]{0:T(1024)(128)(4,1)S(1)}, s32[]{:S(2)}) async-start(s8[16777216]{0:T(1024)(128)(4,1)} %bitcast.292), calls=%async_computation.12 | async-start | bytes 8388608 | tf_op jit(solution)/shard_map/while
  484.7 23.3 %slice-start.2 = ((s8[16777216]{0:T(1024)(128)(4,1)}), s8[4194304]{0:T(1024)(128)(4,1)S(1)}, s32[]{:S(2)}) async-start(s8[16777216]{0:T(1024)(128)(4,1)} %bitcast.292), calls=%async_computation.13 | async-start | bytes 8388608 | tf_op jit(solution)/shard_map/while
  522.8 23.3 %slice-start = ((s8[16777216]{0:T(1024)(128)(4,1)}), s8[4194304]{0:T(1024)(128)(4,1)S(1)}, s32[]{:S(2)}) async-start(s8[16777216]{0:T(1024)(128)(4,1)} %bitcast.292), calls=%async_computation.11 | async-start | bytes 8388608 | tf_op jit(solution)/shard_map/while
  522.8 23.3 %slice-start.1 = ((s8[16777216]{0:T(1024)(128)(4,1)}), s8[4194304]{0:T(1024)(128)(4,1)S(1)}, s32[]{:S(2)}) async-start(s8[16777216]{0:T(1024)(128)(4,1)} %bitcast.292), calls=%async_computation.12 | async-start | bytes 8388608 | tf_op jit(solution)/shard_map/while
  522.8 23.3 %slice-start.2 = ((s8[16777216]{0:T(1024)(128)(4,1)}), s8[4194304]{0:T(1024)(128)(4,1)S(1)}, s32[]{:S(2)}) async-start(s8[16777216]{0:T(1024)(128)(4,1)} %bitcast.292), calls=%async_computation.13 | async-start | bytes 8388608 | tf_op jit(solution)/shard_map/while
  587.8 421.5 %reduce-scatter.5.cloned.1.call-start = ((), (), s32[]{:S(2)}) async-start(), calls=%async_computation.8 | async-start | bytes 25067520 | tf_op jit(solution)/shard_map/reduce_scatter | solution.py:325
  609.5 23.4 %copy-start.22 = (bf16[1024,1024]{0,1:T(8,128)(2,1)S(1)}, bf16[1024,1024]{0,1:T(8,128)(2,1)}, u32[]{:S(2)}) copy-start(bf16[1024,1024]{0,1:T(8,128)(2,1)} %fusion.75) | copy-start | bytes 6291460
  791.0 329.0 %all-gather.22.cloned.1.call-start = ((), (), s32[]{:S(2)}) async-start(), calls=%async_computation.9 | async-start | bytes 13926400 | tf_op jit(solution)/shard_map/all_gather | solution.py:341
  (56 other events, 376.6 us)
Sparse Core Ops, SparseCore 0:
  9.6 36.0 all-gather.11
  65.8 57.8 all-gather.23
  125.3 27.8 all-gather.13
  154.7 59.1 all-gather.15
  215.3 57.9 all-gather.17
  274.7 57.9 all-gather.19
  588.0 69.0 reduce-scatter.2
  791.2 218.1 reduce-scatter.4
  1011.2 108.8 all-gather.21
